TPU v7x, 32 devices: a whole 2x2x4 slice. The times are simulated.
32 devices in a mesh: groups: 2 (over y), shard: 16 (over z, x, core).
Axes of the slice: x: 2, y: 2, z: 4, core: 2. Of those that a mesh axis runs over, the one named last changes fastest.
Arguments:
- grad_out: bfloat16 [4, 4096, 2048], P('groups', 'shard'), parts along dimension 0, may hold values from -6 to 6
- saved_input: bfloat16 [4, 4096, 2048], P('groups', 'shard'), parts along dimension 0, may hold values from -6 to 6
- lengths: int32 [4], P('groups'), parts along dimension 0, may hold values from 1024 to 4096, as said below
- kernel: float32 [31, 2048], replicated, may hold values from -1 to 1
- gain: float32 [2048], replicated, may hold values from 0.1 to 1.9
- bias: float32 [2048], replicated, may hold values from -4 to 4
- proj_weight: bfloat16 [2048, 2048], P('shard'), may hold values from -0.125 to 0.125
Outputs:
- input_grad: bfloat16 [4, 4096, 2048], P('groups', 'shard'), parts along dimension 0
- proj_grad: float32 [4096, 2048], P(('groups', 'shard')), parts along dimension 0
- kernel_grad: float32 [62, 2048], P('groups', 'shard'), parts along dimension 0
- norm_grads: float32 [4, 2048], P('groups', 'shard'), parts along dimension 0
There are 2 independent parts, one for each index of `groups`. A program takes and returns all parts, laid end to end along the dimension named above; an argument that names none is the same for every part. Nothing has to cross between parts.
Inputs may be any that keep to these rules, and one draw needn't show every extreme that they name: `lengths`: one utterance of every microbatch is live over all 4096 frames.
All inputs are finite; a program needn't handle non-finite values.
Results may differ from a plain program's by a relative error of at most 0.0051.
Values may be sent and summed in bfloat16 or wider, within the bound.
No kernel may reach another device: no remote copies, remote signals or barrier semaphores. Data moves between devices by JAX's collectives and lax.ppermute only.
A program may use at most 128 MiB of HBM per device.

v0:
```python
import jax
import jax.numpy as jnp
from jax import lax
from jax.sharding import PartitionSpec as P


def extended(block, sides, width):
    for axis, dim in sides:
        count = lax.axis_size(axis)
        forward = [(i, i + 1) for i in range(count - 1)]
        backward = [(target, source) for source, target in forward]
        low = lax.ppermute(
            lax.slice_in_dim(block, block.shape[dim] - width, None, axis=dim), axis, forward
        )
        high = lax.ppermute(lax.slice_in_dim(block, 0, width, axis=dim), axis, backward)
        block = jnp.concatenate([low, block, high], axis=dim)
    return block


def frame_mask(lengths, offset, count):
    position = offset + jnp.arange(count, dtype=jnp.int32)
    return (position[None, :] < lengths[:, None])[:, :, None]


def forward_taps(padded, kernel, count):
    total = jnp.zeros((padded.shape[0], count, padded.shape[2]), jnp.float32)
    for index_tap in range(kernel.shape[0]):
        total = total + kernel[index_tap] * padded[:, index_tap : index_tap + count, :].astype(
            jnp.float32
        )
    return total


def backward_taps(padded, kernel, count, half_span):
    total = jnp.zeros((padded.shape[0], count, padded.shape[2]), jnp.float32)
    for index_tap in range(kernel.shape[0]):
        begin = 2 * half_span - index_tap
        total = total + kernel[index_tap] * padded[:, begin : begin + count, :].astype(jnp.float32)
    return total


def pre_gradient(act_grad, pre_act, gate_sig):
    return act_grad * gate_sig * (1.0 + pre_act * (1.0 - gate_sig))


def shards(grad_out, saved_input, lengths, kernel, gain, bias, proj_weight):
    batches, frames, model_width = grad_out.shape
    tap_count = kernel.shape[0]
    half_span = (tap_count - 1) // 2
    offset = lax.axis_index("shard") * frames
    norm_scale = lax.rsqrt(jnp.sum(lengths).astype(jnp.float32))
    own_mask = frame_mask(lengths, offset, frames)
    masked_in = jnp.where(own_mask, saved_input, jnp.zeros_like(saved_input))
    masked_grad = jnp.where(own_mask, grad_out, jnp.zeros_like(grad_out))
    in_ext = extended(masked_in, (("shard", 1),), half_span)
    conv = forward_taps(in_ext, kernel, frames)
    pre_act = gain * conv + bias
    gate_sig = jax.nn.sigmoid(pre_act)
    activated = (pre_act * gate_sig).astype(jnp.bfloat16)
    rows = masked_grad.reshape(batches * frames, model_width)
    act_grad = lax.dot_general(
        rows,
        lax.all_gather(proj_weight, "shard", axis=0, tiled=True),
        (((1,), (1,)), ((), ())),
        preferred_element_type=jnp.float32,
    )
    act_grad = act_grad.reshape(batches, frames, model_width)
    pre_grad = pre_gradient(act_grad, pre_act, gate_sig)
    conv_grad = (pre_grad * gain).astype(jnp.bfloat16)
    grad_ext = extended(conv_grad, (("shard", 1),), half_span)
    back_sum = backward_taps(grad_ext, kernel, frames, half_span)
    input_grad = jnp.where(own_mask, back_sum, jnp.zeros_like(back_sum)).astype(jnp.bfloat16)
    grad_float = conv_grad.astype(jnp.float32)
    tap_rows = []
    for index_tap in range(tap_count):
        tap_rows.append(
            jnp.sum(
                in_ext[:, index_tap : index_tap + frames, :].astype(jnp.float32) * grad_float,
                axis=(0, 1),
            )
        )
    gain_term = jnp.sum(pre_grad * conv, axis=(0, 1))
    bias_term = jnp.sum(pre_grad, axis=(0, 1))
    stats = (
        jnp.concatenate([jnp.stack(tap_rows, 0), gain_term[None, :], bias_term[None, :]], 0)
        * norm_scale
    )
    summed = lax.psum_scatter(stats, "shard", scatter_dimension=1, tiled=True)
    act_flat = activated.reshape(batches * frames, model_width)
    grad_flat = masked_grad.reshape(batches * frames, model_width)
    product = lax.dot_general(
        act_flat, grad_flat, (((0,), (0,)), ((), ())), preferred_element_type=jnp.float32
    )
    proj_grad = lax.psum_scatter(product * norm_scale, "shard", scatter_dimension=0, tiled=True)
    return (input_grad, proj_grad, summed[:tap_count], summed[tap_count:])


def solution(mesh):
    placed = (
        P("groups", "shard", None),
        P("groups", "shard", None),
        P("groups"),
        P(),
        P(),
        P(),
        P("shard", None),
    )
    return jax.shard_map(
        shards,
        mesh=mesh,
        in_specs=placed,
        out_specs=(
            P("groups", "shard", None),
            P(("groups", "shard"), None),
            P("groups", "shard"),
            P("groups", "shard"),
        ),
        check_vma=False,
    )
```

profile of v0, /device:TPU:0, one launch (start us, length us, event | category | flops | bytes accessed | tf_op | source)
XLA Modules:
  0.0 358.8 jit_solution(6683365400777504485)
XLA Ops:
  7.2 0.0 copy-start.4
  7.2 0.0 copy-start.3
  7.2 0.0 all-gather.2.cloned.1.call-start
  7.2 0.7 all-gather.2.cloned.1.call-update
  7.9 0.0 reduce-scatter.5.cloned.1.call-start
  8.0 0.7 broadcast_compare_fusion
  8.7 1.8 broadcast_select_fusion
  10.5 0.0 copy-start.5
  10.5 0.0 copy-start.6
  10.6 2.4 collective-permute-start
  13.0 1.3 collective-permute-start.1
  14.3 0.0 copy-done.3
  14.3 0.1 fusion.148
  14.4 0.1 fusion.149
  14.5 0.0 copy-done.4
  14.5 0.6 reduce_sum.306
  15.8 0.0 collective-permute-done
  15.9 2.5 collective-permute-done.1
  18.3 19.8 %fusion.31 = f32[2,256,2048]{2,1,0:T(8,128)} fusion(bf16[2,256,2048]{2,1,0:T(8,128)(2,1)S(1)} %broadcast_select_fusion, bf16[2,15,2048]{2,1,0:T(8,128)(2,1)S(1)} %collective-permute-done.1, bf16[2,15,2048]{2,1,0:T(8,128)(2,1)S(1)} %collective-permute-done, f32[2048]{0:T(1024)S(1)} %bitcast.131, f32[2048]{0:T(1024)S(1)} %bitcast.133, f32[2048]{0:T(1024)S(1)} %bitcast.75, ...), kind=kLoop, calls=%fused_computation.151 | loop fusion | flops 190840832 | bytes 6791168 | tf_op jit(solution)/shard_map/add | solution.py:28
  38.2 49.0 %all-gather.2.cloned.1.call-done = bf16[2048,2048]{1,0:T(8,128)(2,1)} async-done(((bf16[128,2048]{1,0:T(8,128)(2,1)}), bf16[2048,2048]{1,0:T(8,128)(2,1)}) %all-gather.2.cloned.1.call-update) | async-done | bytes 8388624 | tf_op jit(solution)/shard_map/all_gather | solution.py:63
  87.2 0.0 copy-done.5
  87.2 0.0 copy-done.6
  87.2 0.0 copy-start.2
  87.2 16.0 %fusion.78 = (f32[2048]{0:T(1024)S(1)}, f32[2048]{0:T(1024)S(1)}, f32[2048]{0:T(1024)S(1)}, f32[2048]{0:T(1024)S(1)}, f32[2048]{0:T(1024)S(1)}, /*index=5*/f32[2...) fusion(bf16[2,15,2048]{2,1,0:T(8,128)(2,1)S(1)} %collective-per, ...), kind=kOutput, calls=%fused_computation.198 | convolution fusion | flops 4366252032 | bytes 23282176 | tf_op jit(solution)/shard_map/dot_general | solution.py:61
  103.2 0.0 copy-start
  103.2 0.0 copy-done.2
  103.3 1.2 fusion.145
  104.4 5.0 %fusion.77 = (f32[2048]{0:T(1024)S(1)}, f32[2048]{0:T(1024)S(1)}, f32[2048]{0:T(1024)S(1)}, f32[2048]{0:T(1024)S(1)}, f32[2048]{0:T(1024)S(1)}, /*index=5*/f32[2048]{0:T(1024)S(1)}, f32[2048]{0:T(1024)S(1)}) fusion(bf16[2,256,2048]{2,1,0:T(8,128)(2,1)S(1)} %get-tuple-element.37, bf16[2,15,2048]{2,1,0:T(8,128)(2,1)S(1)} %collective-permute-done.1, ...), kind=kLoop, calls=%fused_computation.197 | loop fusion | flops 41928704 | bytes 4374528 | tf_op jit(solution)/shard_map/reduce_sum | solution.py:77
  109.5 3.9 %fusion.61 = (f32[2048]{0:T(1024)S(1)}, f32[2048]{0:T(1024)S(1)}, f32[2048]{0:T(1024)S(1)}, f32[2048]{0:T(1024)S(1)}, f32[2048]{0:T(1024)S(1)}, /*index=5*/f32[2048]{0:T(1024)S(1)}) fusion(bf16[2,256,2048]{2,1,0:T(8,128)(2,1)S(1)} %get-tuple-element.37, bf16[2,256,2048]{2,1,0:T(8,128)(2,1)S(1)} %broadcast_select_fusion, ...), kind=kLoop, calls=%fused_computation.181 | loop fusion | flops 38785024 | bytes 4366336 | tf_op jit(solution)/shard_map/reduce_sum | solution.py:77
  113.4 0.0 copy-done
  113.4 5.4 %fusion.62 = (f32[2048]{0:T(1024)S(1)}, f32[2048]{0:T(1024)S(1)}, f32[2048]{0:T(1024)S(1)}, f32[2048]{0:T(1024)S(1)}, f32[2048]{0:T(1024)S(1)}, /*index=5*/f32[2...) fusion(bf16[2,256,2048]{2,1,0:T(8,128)(2,1)S(1)} %get-tuple-element.37, ...), kind=kLoop, calls=%fused_computation.182 | loop fusion | flops 57653248 | bytes 4390912 | tf_op jit(solution)/shard_map/reduce_sum | solution.py:77
  118.8 0.4 concatenate.77
  119.3 0.8 broadcast_multiply_fusion
  120.0 0.0 reduce-scatter.5.cloned.1.call-update
  120.0 0.2 reduce-scatter.3.cloned.1.call-start
  120.3 13.6 %bitcast_multiply_fusion = f32[2048,2048]{1,0:T(8,128)} fusion(f32[]{:T(128)S(6)} %rsqrt.3, f32[2,256,2048]{2,1,0:T(8,128)} %fusion.31, f32[2048]{0:T(1024)S(1)} %copy-done.6, f32[2048]{0:T(1024)S(1)} %copy-done.5, bf16[2,256,2048]{2,1,0:T(8,128)(2,1)} %param.7, pred[2,256]{1,0:T(4,128)(4,1)S(1)} %broadcast_compare_fusion), kind=kOutput, calls=%fused_computation.32 | convolution fusion | flops 4307550208 | bytes 23085572 | tf_op jit(solution)/shard_map/dot_general | solution.py:91
  133.8 0.0 copy-start.1
  133.9 0.0 reduce-scatter.3.cloned.1.call-update
  133.9 1.6 copy-done.1
  135.5 1.3 collective-permute-start.2
  136.8 3.0 collective-permute-start.3
  139.8 0.0 collective-permute-done.2
  139.8 1.0 collective-permute-done.3
  140.8 32.7 %select_convert_fusion = bf16[2,256,2048]{2,1,0:T(8,128)(2,1)} fusion(bf16[2,256,2048]{2,1,0:T(8,128)(2,1)S(1)} %copy-done.1, bf16[2,15,2048]{2,1,0:T(8,128)(2,1)S(1)} %collective-permute-done.3, bf16[2,15,2048]{2,1,0:T(8,128)(2,1)S(1)} %collective-permute-done.2, f32[2048]{0:T(1024)S(1)} %bitcast.132, f32[2048]{0:T(1024)S(1)} %bitcast.134, ...), kind=kLoop, calls=%fused_computation.201 | loop fusion | flops 192937984 | bytes 4694528 | tf_op jit(solution)/shard_map/convert_element_type | solution.py:72
  173.5 0.0 reduce-scatter.5.cloned.1.call-done
  173.5 1.3 slice.626
  174.8 1.3 slice.625
  176.1 176.2 %reduce-scatter.3.cloned.1.call-done = f32[128,2048]{1,0:T(8,128)} async-done(((f32[2048,2048]{1,0:T(8,128)}), f32[128,2048]{1,0:T(8,128)}) %reduce-scatter.3.cloned.1.call-update) | async-done | bytes 1048592 | tf_op jit(solution)/shard_map/reduce_scatter | solution.py:94
  (3 shorter events, 0.1 us)
Async XLA Ops:
  7.2 7.3 %copy-start.4 = (s32[2]{0:T(128)S(1)}, s32[2]{0:T(128)}, u32[]{:S(2)}) copy-start(s32[2]{0:T(128)} %param.9) | copy-start | bytes 28
  7.2 7.1 %copy-start.3 = (f32[31,2048]{1,0:T(8,128)S(1)}, f32[31,2048]{1,0:T(8,128)}, u32[]{:S(2)}) copy-start(f32[31,2048]{1,0:T(8,128)} %param.10) | copy-start | bytes 761860
  7.2 80.0 %all-gather.2.cloned.1.call-start = ((), (), s32[]{:S(2)}) async-start(), calls=%async_computation.2 | async-start | bytes 8912896 | tf_op jit(solution)/shard_map/all_gather | solution.py:63
  7.9 165.6 %reduce-scatter.5.cloned.1.call-start = ((), (), s32[]{:S(2)}) async-start(), calls=%async_computation.4 | async-start | bytes 348160 | tf_op jit(solution)/shard_map/reduce_scatter | solution.py:88
  10.5 76.7 %copy-start.5 = (f32[2048]{0:T(1024)S(1)}, f32[2048]{0:T(1024)}, u32[]{:S(2)}) copy-start(f32[2048]{0:T(1024)} %param.11) | copy-start | bytes 24580
  10.5 76.7 %copy-start.6 = (f32[2048]{0:T(1024)S(1)}, f32[2048]{0:T(1024)}, u32[]{:S(2)}) copy-start(f32[2048]{0:T(1024)} %param.12) | copy-start | bytes 24580
  10.6 5.3 %collective-permute-start = (bf16[2,15,2048]{2,1,0:T(8,128)(2,1)S(1)}, bf16[2,15,2048]{2,1,0:T(8,128)(2,1)S(1)}, u32[]{:S(2)}, u32[]{:S(2)}) collective-permute-start(bf16[2,15,2048]{2,1,0:T(8,128)(2,1)S(1)} %get-tuple-element.40), channel_id=1, source_target_pairs={{0,1},{1,2},{2,3},{3,4},{4,5},{5,6},{6,7},{7,8},{8,9},{9,10},{10,1... | collective-permute-start | bytes 368648 | tf_op jit(solution)/shard_map/ppermute | solution.py:12
  13.0 5.3 %collective-permute-start.1 = (bf16[2,15,2048]{2,1,0:T(8,128)(2,1)S(1)}, bf16[2,15,2048]{2,1,0:T(8,128)(2,1)S(1)}, u32[]{:S(2)}, u32[]{:S(2)}) collective-permute-start(bf16[2,15,2048]{2,1,0:T(8,128)(2,1)S(1)} %get-tuple-element.41), channel_id=1, source_target_pairs={{1,0},{2,1},{3,2},{4,3},{5,4},{6,5},{7,6},{8,7},{9,8},{10,9},{11,1... | collective-permute-start | bytes 368648 | tf_op jit(solution)/shard_map/ppermute | solution.py:15
  87.2 16.0 %copy-start.2 = (f32[2,256,2048]{2,1,0:T(8,128)S(1)}, f32[2,256,2048]{2,1,0:T(8,128)}, u32[]{:S(2)}) copy-start(f32[2,256,2048]{2,1,0:T(8,128)} %fusion.31) | copy-start | bytes 12582916
  103.2 10.1 %copy-start = (bf16[2,256,2048]{2,1,0:T(8,128)(2,1)}, bf16[2,256,2048]{2,1,0:T(8,128)(2,1)S(1)}, u32[]{:S(2)}) copy-start(bf16[2,256,2048]{2,1,0:T(8,128)(2,1)S(1)} %get-tuple-element.37) | copy-start | bytes 6291460
  120.0 232.3 %reduce-scatter.3.cloned.1.call-start = ((), (), s32[]{:S(2)}) async-start(), calls=%async_computation.3 | async-start | bytes 17825792 | tf_op jit(solution)/shard_map/reduce_scatter | solution.py:94
  133.8 1.6 copy-start.1
  135.5 4.3 %collective-permute-start.2 = (bf16[2,15,2048]{2,1,0:T(8,128)(2,1)S(1)}, bf16[2,15,2048]{2,1,0:T(8,128)(2,1)S(1)}, u32[]{:S(2)}, u32[]{:S(2)}) collective-permute-start(bf16[2,15,2048]{2,1,0:T(8,128)(2,1)S(1)} %get-tuple-element.38), channel_id=1, source_target_pairs={{1,0},{2,1},{3,2},{4,3},{5,4},{6,5},{7,6},{8,7},{9,8},{10,9},{11,1... | collective-permute-start | bytes 368648 | tf_op jit(solution)/shard_map/ppermute | solution.py:15
  136.8 4.0 %collective-permute-start.3 = (bf16[2,15,2048]{2,1,0:T(8,128)(2,1)S(1)}, bf16[2,15,2048]{2,1,0:T(8,128)(2,1)S(1)}, u32[]{:S(2)}, u32[]{:S(2)}) collective-permute-start(bf16[2,15,2048]{2,1,0:T(8,128)(2,1)S(1)} %get-tuple-element.39), channel_id=1, source_target_pairs={{0,1},{1,2},{2,3},{3,4},{4,5},{5,6},{6,7},{7,8},{8,9},{9,10},{10,1... | collective-permute-start | bytes 368648 | tf_op jit(solution)/shard_map/ppermute | solution.py:12
Sparse Core Ops, SparseCore 0:
  10.2 77.0 all-gather.1
  120.2 50.9 reduce-scatter.4
  175.9 176.3 reduce-scatter.2
where the time goes:
time: 359 us
  waiting for transfers between devices  229 us (64%)
  other arithmetic  72 us (20%)
  matrix products  29.6 us (8%)
  between operations  14.6 us (4%)
  starting transfers between devices  8.32 us (2%)
  local copies, waits for them, and re-layouts  4.89 us (1%)
    reduce_scatter x1, waiting for transfers between devices, shards(): lax.psum_scatter(product * norm_scale, 'shard', scatter_dimension=0, tile...  176 us
    all_gather x1, waiting for transfers between devices, shards(): lax.all_gather(proj_weight, 'shard', axis=0, tiled=True)  49 us
    convert_element_type x1, other arithmetic, shards(): jnp.where(own_mask, back_sum, jnp.zeros_like(back_sum)).astype(jnp.bfloat16)  32.7 us
    add x1, other arithmetic, forward_taps(): total + kernel[index_tap] * padded[:, index_tap:index_tap + count, :].ast...  19.8 us
    dot_general x1, matrix products, shards(): lax.dot_general(rows, lax.all_gather(proj_weight, 'shard', axis=0, tiled=...  16 us
    reduce_sum x3, other arithmetic, shards(): jnp.sum(in_ext[:, index_tap:index_tap + frames, :].astype(jnp.float32) *...  14.4 us
    dot_general x1, matrix products, shards(): lax.dot_general(act_flat, grad_flat, (((0,), (0,)), ((), ())), preferred_...  13.6 us
  transfers between devices with their start and end apart: 7, of which 4 were waited for; matrix products, arithmetic and copies ran while one was open for 20% of the time, Pallas kernels for 0%

commit v1 on v0

--- a/solution.py
+++ b/solution.py
@@ -2,6 +2,25 @@
 import jax.numpy as jnp
 from jax import lax
 from jax.sharding import PartitionSpec as P
+
+
+def gather_around(x, axis, dim):
+    size, place, span = (lax.axis_size(axis), lax.axis_index(axis), x.shape[dim])
+    ahead = [(i, (i + 1) % size) for i in range(size)]
+    left = [(i, (i - 1) % size) for i in range(size)]
+    out = jnp.zeros((*x.shape[:dim], size * span, *x.shape[dim + 1 :]), x.dtype)
+    out = lax.dynamic_update_slice_in_dim(out, x, place * span, axis=dim)
+    from_left = from_right = x
+    middle = size // 2
+    for hop in range(1, middle + 1):
+        from_left = lax.ppermute(from_left, axis, ahead)
+        out = lax.dynamic_update_slice_in_dim(out, from_left, (place - hop) % size * span, axis=dim)
+        if hop < size - middle:
+            from_right = lax.ppermute(from_right, axis, left)
+            out = lax.dynamic_update_slice_in_dim(
+                out, from_right, (place + hop) % size * span, axis=dim
+            )
+    return out
 
 
 def extended(block, sides, width):
@@ -60,7 +79,7 @@
     rows = masked_grad.reshape(batches * frames, model_width)
     act_grad = lax.dot_general(
         rows,
-        lax.all_gather(proj_weight, "shard", axis=0, tiled=True),
+        gather_around(proj_weight, "shard", 0),
         (((1,), (1,)), ((), ())),
         preferred_element_type=jnp.float32,
     )

time: 359 us -> 406 us (1.13)
  starting transfers between devices: 8.32 us -> 69.3 us
  waiting for transfers between devices: 229 us -> 184 us
  local copies, waits for them, and re-layouts: 4.89 us -> 32.9 us
    ppermute x0 -> x15, starting transfers between devices: none -> 53.4 us  [the longest x8 35.6 us: gather_around(): from_left = lax.ppermute(from_left, axis, ahead)]
    all_gather x1 -> x0, waiting for transfers between devices: 49 us -> none  [shards(): lax.all_gather(proj_weight, 'shard', axis=0, tiled=True)]
    dynamic_update_slice x0 -> x16, local copies, waits for them, and re-layouts: none -> 18.8 us  [the longest x8 9.93 us: gather_around(): lax.dynamic_update_slice_in_dim(out, from_left, (place - hop) % size * sp...]
    ppermute x2, starting transfers between devices: 5.44 us -> 13 us  [extended(): lax.ppermute(lax.slice_in_dim(block, block.shape[dim] - width, None, axis...]
    ppermute x0 -> x15, waiting for transfers between devices: none -> 6.77 us  [the longest x8 6.75 us: gather_around(): from_left = lax.ppermute(from_left, axis, ahead)]
    broadcast_in_dim x0 -> x1, local copies, waits for them, and re-layouts: none -> 4.29 us  [gather_around(): out = jnp.zeros((*x.shape[:dim], size * span, *x.shape[dim + 1:]), x.dtype)]
  transfers between devices with their start and end apart: 7 -> 21, of which waited for: 4 -> 7; matrix products, arithmetic and copies ran while one was open for 20% -> 25% of each run, Pallas kernels for 0% -> 0%
where the time goes in v1:
time: 406 us; the launch traced here: 405 us
  waiting for transfers between devices  184 us (45%)
  other arithmetic  75 us (18%)
  starting transfers between devices  69.3 us (17%)
  local copies, waits for them, and re-layouts  32.9 us (8%)
  matrix products  28 us (7%)
  between operations  15.7 us (4%)
    reduce_scatter x1, waiting for transfers between devices, shards(): lax.psum_scatter(product * norm_scale, 'shard', scatter_dimension=0, tile...  177 us
    ppermute x8, starting transfers between devices, gather_around(): from_left = lax.ppermute(from_left, axis, ahead)  35.6 us
    convert_element_type x1, other arithmetic, shards(): jnp.where(own_mask, back_sum, jnp.zeros_like(back_sum)).astype(jnp.bfloat16)  32.7 us
    add x1, other arithmetic, forward_taps(): total + kernel[index_tap] * padded[:, index_tap:index_tap + count, :].ast...  22.9 us
    ppermute x7, starting transfers between devices, gather_around(): from_right = lax.ppermute(from_right, axis, left)  17.8 us
    dot_general x1, matrix products, shards(): lax.dot_general(rows, gather_around(proj_weight, 'shard', 0), (((1,), (1,...  14.5 us
    reduce_sum x3, other arithmetic, shards(): jnp.sum(in_ext[:, index_tap:index_tap + frames, :].astype(jnp.float32) *...  14.4 us
    dot_general x1, matrix products, shards(): lax.dot_general(act_flat, grad_flat, (((0,), (0,)), ((), ())), preferred_...  13.6 us
  transfers between devices with their start and end apart: 21, of which 7 were waited for; matrix products, arithmetic and copies ran while one was open for 25% of the time, Pallas kernels for 0%

profile of v1, /device:TPU:0, one launch (start us, length us, event | category | flops | bytes accessed | tf_op | source)
XLA Modules:
  0.0 405.3 jit_solution(15079625928451379297)
XLA Ops:
  7.8 5.0 %collective-permute-start.1 = (bf16[128,2048]{1,0:T(8,128)(2,1)}, bf16[128,2048]{1,0:T(8,128)(2,1)S(1)}, u32[]{:S(2)}, u32[]{:S(2)}) collective-permute-start(bf16[128,2048]{1,0:T(8,128)(2,1)} %param.13), channel_id=1, source_target_pairs={{0,15},{1,0},{2,1},{3,2},{4,3},{5,4},{6,5},{7,6},{8,7},{9,8},{10,9... | collective-permute-start | bytes 1572872 | tf_op jit(solution)/shard_map/ppermute | solution.py:19
  13.5 1.8 broadcast_select_fusion
  15.3 4.6 %collective-permute-done = bf16[128,2048]{1,0:T(8,128)(2,1)S(1)} collective-permute-done((bf16[128,2048]{1,0:T(8,128)(2,1)}, bf16[128,2048]{1,0:T(8,128)(2,1)S(1)}, u32[]{:S(2)}, u32[]{:S(2)}) %collective-permute-start) | collective-permute-done | bytes 524320 | tf_op jit(solution)/shard_map/ppermute | solution.py:16
  19.9 2.5 collective-permute-start.2
  23.1 4.3 %collective-permute-start.15 = (bf16[2,15,2048]{2,1,0:T(8,128)(2,1)}, bf16[2,15,2048]{2,1,0:T(8,128)(2,1)S(1)}, u32[]{:S(2)}, u32[]{:S(2)}) collective-permute-start(bf16[2,15,2048]{2,1,0:T(8,128)(2,1)} %get-tuple-element.40), channel_id=1, source_target_pairs={{0,1},{1,2},{2,3},{3,4},{4,5},{5,6},{6,7},{7,8},{8,9},{9,10},{10,1... | collective-permute-start | bytes 368648 | tf_op jit(solution)/shard_map/ppermute | solution.py:31
  27.4 1.3 collective-permute-start.16
  30.4 2.5 fusion.148
  32.9 3.7 collective-permute-start.3
  36.6 2.1 fusion.149
  38.7 4.3 %broadcast_in_dim.36 = bf16[2048,2048]{1,0:T(8,128)(2,1)} broadcast(bf16[]{:T(256)} %constant.96.clone.1), dimensions={} | broadcast | bytes 8388610 | tf_op jit(solution)/shard_map/broadcast_in_dim | solution.py:11
  43.0 0.8 constant_dynamic-update-slice_fusion.15
  43.8 4.5 %collective-permute-start.5 = (bf16[128,2048]{1,0:T(8,128)(2,1)}, bf16[128,2048]{1,0:T(8,128)(2,1)}, u32[]{:S(2)}, u32[]{:S(2)}) collective-permute-start(bf16[128,2048]{1,0:T(8,128)(2,1)} %collective-permute-done.3), channel_id=1, source_target_pairs={{0,15},{1,0},{2,1},{3,2},{4,3},{5,4},{6,5},{7,6},{8,7},{9,8},{10,9... | collective-permute-start | bytes 1572872 | tf_op jit(solution)/shard_map/ppermute | solution.py:19
  48.3 4.7 %collective-permute-start.6 = (bf16[128,2048]{1,0:T(8,128)(2,1)}, bf16[128,2048]{1,0:T(8,128)(2,1)}, u32[]{:S(2)}, u32[]{:S(2)}) collective-permute-start(bf16[128,2048]{1,0:T(8,128)(2,1)} %collective-permute-done.4), channel_id=1, source_target_pairs={{0,1},{1,2},{2,3},{3,4},{4,5},{5,6},{6,7},{7,8},{8,9},{9,10},{10,1... | collective-permute-start | bytes 1572872 | tf_op jit(solution)/shard_map/ppermute | solution.py:16
  53.0 22.9 %fusion.31 = f32[2,256,2048]{2,1,0:T(8,128)} fusion(bf16[2,256,2048]{2,1,0:T(8,128)(2,1)S(1)} %broadcast_select_fusion, bf16[2,15,2048]{2,1,0:T(8,128)(2,1)S(1)} %collective-permute-done.16, bf16[2,15,2048]{2,1,0:T(8,128)(2,1)S(1)} %collective-permute-done.15, f32[2048]{0:T(1024)} %bitcast.131, f32[2048]{0:T(1024)} %bitcast.133, f32[2048]{0:T(1024)S(1)} %bitcast.75, ...), kind=kLoop, calls=%fused_computation.151 | loop fusion | flops 190840832 | bytes 6791168 | tf_op jit(solution)/shard_map/add | solution.py:47
  75.9 0.9 constant_dynamic-update-slice_fusion.14
  76.8 0.9 constant_dynamic-update-slice_fusion.13
  77.6 2.5 collective-permute-start.8
  80.1 1.9 constant_dynamic-update-slice_fusion.12
  82.0 1.9 constant_dynamic-update-slice_fusion.11
  83.9 4.5 %collective-permute-start.9 = (bf16[128,2048]{1,0:T(8,128)(2,1)S(1)}, bf16[128,2048]{1,0:T(8,128)(2,1)S(1)}, u32[]{:S(2)}, u32[]{:S(2)}) collective-permute-start(bf16[128,2048]{1,0:T(8,128)(2,1)S(1)} %collective-permute-done.7), channel_id=1, source_target_pairs={{0,15},{1,0},{2,1},{3,2},{4,3},{5,4},{6,5},{7,6},{8,7},{9,8},{10,9... | collective-permute-start | bytes 1572872 | tf_op jit(solution)/shard_map/ppermute | solution.py:19
  88.4 1.9 constant_dynamic-update-slice_fusion.10
  90.3 5.9 %collective-permute-start.10 = (bf16[128,2048]{1,0:T(8,128)(2,1)S(1)}, bf16[128,2048]{1,0:T(8,128)(2,1)S(1)}, u32[]{:S(2)}, u32[]{:S(2)}) collective-permute-start(bf16[128,2048]{1,0:T(8,128)(2,1)S(1)} %collective-permute-done.8), channel_id=1, source_target_pairs={{0,1},{1,2},{2,3},{3,4},{4,5},{5,6},{6,7},{7,8},{8,9},{9,10},{10,1... | collective-permute-start | bytes 1572872 | tf_op jit(solution)/shard_map/ppermute | solution.py:16
  96.2 1.9 constant_dynamic-update-slice_fusion.9
  98.1 1.9 constant_dynamic-update-slice_fusion.8
  100.0 0.9 constant_dynamic-update-slice_fusion.7
  101.7 8.6 %collective-permute-start.12 = (bf16[128,2048]{1,0:T(8,128)(2,1)S(1)}, bf16[128,2048]{1,0:T(8,128)(2,1)S(1)}, u32[]{:S(2)}, u32[]{:S(2)}) collective-permute-start(bf16[128,2048]{1,0:T(8,128)(2,1)S(1)} %collective-permute-done.10), channel_id=1, source_target_pairs={{0,1},{1,2},{2,3},{3,4},{4,5},{5,6},{6,7},{7,8},{8,9},{9,10},{10,1... | collective-permute-start | bytes 1572872 | tf_op jit(solution)/shard_map/ppermute | solution.py:16
  110.3 0.9 constant_dynamic-update-slice_fusion.6
  111.1 0.8 constant_dynamic-update-slice_fusion.5
  112.0 0.8 constant_dynamic-update-slice_fusion.4
  113.5 11.0 %collective-permute-start.14 = (bf16[128,2048]{1,0:T(8,128)(2,1)S(1)}, bf16[128,2048]{1,0:T(8,128)(2,1)S(1)}, u32[]{:S(2)}, u32[]{:S(2)}) collective-permute-start(bf16[128,2048]{1,0:T(8,128)(2,1)S(1)} %collective-permute-done.12), channel_id=1, source_target_pairs={{0,1},{1,2},{2,3},{3,4},{4,5},{5,6},{6,7},{7,8},{8,9},{9,10},{10,1... | collective-permute-start | bytes 1572872 | tf_op jit(solution)/shard_map/ppermute | solution.py:16
  124.5 0.8 constant_dynamic-update-slice_fusion.3
  125.3 0.9 constant_dynamic-update-slice_fusion.2
  126.2 0.9 constant_dynamic-update-slice_fusion.1
  127.7 0.8 constant_dynamic-update-slice_fusion
  128.5 14.5 %fusion.78 = (f32[2048]{0:T(1024)S(1)}, f32[2048]{0:T(1024)S(1)}, f32[2048]{0:T(1024)S(1)}, f32[2048]{0:T(1024)S(1)}, f32[2048]{0:T(1024)S(1)}, /*index=5*/f32[2...) fusion(bf16[2,15,2048]{2,1,0:T(8,128)(2,1)S(1)} %collective-per, ...), kind=kOutput, calls=%fused_computation.198 | convolution fusion | flops 4366252032 | bytes 23282176 | tf_op jit(solution)/shard_map/dot_general | solution.py:80
  143.1 1.2 fusion.145
  144.2 5.4 %fusion.62 = (f32[2048]{0:T(1024)S(1)}, f32[2048]{0:T(1024)S(1)}, f32[2048]{0:T(1024)S(1)}, f32[2048]{0:T(1024)S(1)}, f32[2048]{0:T(1024)S(1)}, /*index=5*/f32[2...) fusion(bf16[2,256,2048]{2,1,0:T(8,128)(2,1)S(1)} %get-tuple-element.37, ...), kind=kLoop, calls=%fused_computation.182 | loop fusion | flops 57653248 | bytes 4390912 | tf_op jit(solution)/shard_map/reduce_sum | solution.py:96
  149.7 5.0 %fusion.77 = (f32[2048]{0:T(1024)S(1)}, f32[2048]{0:T(1024)S(1)}, f32[2048]{0:T(1024)S(1)}, f32[2048]{0:T(1024)S(1)}, f32[2048]{0:T(1024)S(1)}, /*index=5*/f32[2048]{0:T(1024)S(1)}, f32[2048]{0:T(1024)S(1)}) fusion(bf16[2,256,2048]{2,1,0:T(8,128)(2,1)S(1)} %get-tuple-element.37, bf16[2,15,2048]{2,1,0:T(8,128)(2,1)S(1)} %collective-permute-done.16, ...), kind=kLoop, calls=%fused_computation.197 | loop fusion | flops 41928704 | bytes 4374528 | tf_op jit(solution)/shard_map/reduce_sum | solution.py:96
  154.7 3.9 fusion.61
  160.1 13.6 %bitcast_multiply_fusion = f32[2048,2048]{1,0:T(8,128)} fusion(f32[]{:T(128)S(6)} %rsqrt.3, f32[2,256,2048]{2,1,0:T(8,128)} %fusion.31, f32[2048]{0:T(1024)S(1)} %copy-done.38, f32[2048]{0:T(1024)S(1)} %copy-done.37, bf16[2,256,2048]{2,1,0:T(8,128)(2,1)} %param.7, pred[2,256]{1,0:T(4,128)(4,1)S(1)} %copy-done.34), kind=kOutput, calls=%fused_computation.32 | convolution fusion | flops 4307550208 | bytes 23085572 | tf_op jit(solution)/shard_map/dot_general | solution.py:110
  174.0 1.3 copy-done.1
  175.3 1.3 collective-permute-start.17
  176.6 8.7 %collective-permute-start.18 = (bf16[2,15,2048]{2,1,0:T(8,128)(2,1)S(1)}, bf16[2,15,2048]{2,1,0:T(8,128)(2,1)S(1)}, u32[]{:S(2)}, u32[]{:S(2)}) collective-permute-start(bf16[2,15,2048]{2,1,0:T(8,128)(2,1)S(1)} %get-tuple-element.39), channel_id=1, source_target_pairs={{0,1},{1,2},{2,3},{3,4},{4,5},{5,6},{6,7},{7,8},{8,9},{9,10},{10,1... | collective-permute-start | bytes 368648 | tf_op jit(solution)/shard_map/ppermute | solution.py:31
  185.4 1.0 collective-permute-done.18
  186.6 32.7 %select_convert_fusion = bf16[2,256,2048]{2,1,0:T(8,128)(2,1)} fusion(bf16[2,256,2048]{2,1,0:T(8,128)(2,1)S(1)} %copy-done.1, bf16[2,15,2048]{2,1,0:T(8,128)(2,1)S(1)} %collective-permute-done.18, bf16[2,15,2048]{2,1,0:T(8,128)(2,1)S(1)} %collective-permute-done.17, f32[2048]{0:T(1024)S(1)} %bitcast.132, f32[2048]{0:T(1024)S(1)} %bitcast.134, ...), kind=kLoop, calls=%fused_computation.201 | loop fusion | flops 192937984 | bytes 4694528 | tf_op jit(solution)/shard_map/convert_element_type | solution.py:91
  219.3 1.3 slice.625
  220.6 1.3 slice.626
  221.9 176.6 %reduce-scatter.3.cloned.1.call-done = f32[128,2048]{1,0:T(8,128)} async-done(((f32[2048,2048]{1,0:T(8,128)}), f32[128,2048]{1,0:T(8,128)}) %reduce-scatter.3.cloned.1.call-update) | async-done | bytes 1048592 | tf_op jit(solution)/shard_map/reduce_scatter | solution.py:113
  (111 shorter events, 6.6 us)
Async XLA Ops:
  7.2 21.8 %copy-start.35 = (s32[2]{0:T(128)S(1)}, s32[2]{0:T(128)}, u32[]{:S(2)}) copy-start(s32[2]{0:T(128)} %param.9) | copy-start | bytes 28
  7.2 212.1 %reduce-scatter.5.cloned.1.call-start = ((), (), s32[]{:S(2)}) async-start(), calls=%async_computation.3 | async-start | bytes 348160 | tf_op jit(solution)/shard_map/reduce_scatter | solution.py:107
  7.2 12.7 %collective-permute-start = (bf16[128,2048]{1,0:T(8,128)(2,1)}, bf16[128,2048]{1,0:T(8,128)(2,1)S(1)}, u32[]{:S(2)}, u32[]{:S(2)}) collective-permute-start(bf16[128,2048]{1,0:T(8,128)(2,1)} %param.13), channel_id=1, source_target_pairs={{0,1},{1,2},{2,3},{3,4},{4,5},{5,6},{6,7},{7,8},{8,9},{9,10},{10,1... | collective-permute-start | bytes 1572872 | tf_op jit(solution)/shard_map/ppermute | solution.py:16
  7.8 25.1 %collective-permute-start.1 = (bf16[128,2048]{1,0:T(8,128)(2,1)}, bf16[128,2048]{1,0:T(8,128)(2,1)S(1)}, u32[]{:S(2)}, u32[]{:S(2)}) collective-permute-start(bf16[128,2048]{1,0:T(8,128)(2,1)} %param.13), channel_id=1, source_target_pairs={{0,15},{1,0},{2,1},{3,2},{4,3},{5,4},{6,5},{7,6},{8,7},{9,8},{10,9... | collective-permute-start | bytes 1572872 | tf_op jit(solution)/shard_map/ppermute | solution.py:19
  19.9 16.7 %collective-permute-start.2 = (bf16[128,2048]{1,0:T(8,128)(2,1)S(1)}, bf16[128,2048]{1,0:T(8,128)(2,1)}, u32[]{:S(2)}, u32[]{:S(2)}) collective-permute-start(bf16[128,2048]{1,0:T(8,128)(2,1)S(1)} %collective-permute-done), channel_id=1, source_target_pairs={{0,1},{1,2},{2,3},{3,4},{4,5},{5,6},{6,7},{7,8},{8,9},{9,10},{10,1... | collective-permute-start | bytes 1572872 | tf_op jit(solution)/shard_map/ppermute | solution.py:16
  23.1 29.9 %collective-permute-start.15 = (bf16[2,15,2048]{2,1,0:T(8,128)(2,1)}, bf16[2,15,2048]{2,1,0:T(8,128)(2,1)S(1)}, u32[]{:S(2)}, u32[]{:S(2)}) collective-permute-start(bf16[2,15,2048]{2,1,0:T(8,128)(2,1)} %get-tuple-element.40), channel_id=1, source_target_pairs={{0,1},{1,2},{2,3},{3,4},{4,5},{5,6},{6,7},{7,8},{8,9},{9,10},{10,1... | collective-permute-start | bytes 368648 | tf_op jit(solution)/shard_map/ppermute | solution.py:31
  27.4 25.6 %collective-permute-start.16 = (bf16[2,15,2048]{2,1,0:T(8,128)(2,1)S(1)}, bf16[2,15,2048]{2,1,0:T(8,128)(2,1)S(1)}, u32[]{:S(2)}, u32[]{:S(2)}) collective-permute-start(bf16[2,15,2048]{2,1,0:T(8,128)(2,1)S(1)} %get-tuple-element.41), channel_id=1, source_target_pairs={{1,0},{2,1},{3,2},{4,3},{5,4},{6,5},{7,6},{8,7},{9,8},{10,9},{11,1... | collective-permute-start | bytes 368648 | tf_op jit(solution)/shard_map/ppermute | solution.py:34
  32.9 10.9 %collective-permute-start.3 = (bf16[128,2048]{1,0:T(8,128)(2,1)S(1)}, bf16[128,2048]{1,0:T(8,128)(2,1)}, u32[]{:S(2)}, u32[]{:S(2)}) collective-permute-start(bf16[128,2048]{1,0:T(8,128)(2,1)S(1)} %collective-permute-done.1), channel_id=1, source_target_pairs={{0,15},{1,0},{2,1},{3,2},{4,3},{5,4},{6,5},{7,6},{8,7},{9,8},{10,9... | collective-permute-start | bytes 1572872 | tf_op jit(solution)/shard_map/ppermute | solution.py:19
  36.6 11.7 %collective-permute-start.4 = (bf16[128,2048]{1,0:T(8,128)(2,1)}, bf16[128,2048]{1,0:T(8,128)(2,1)}, u32[]{:S(2)}, u32[]{:S(2)}) collective-permute-start(bf16[128,2048]{1,0:T(8,128)(2,1)} %collective-permute-done.2), channel_id=1, source_target_pairs={{0,1},{1,2},{2,3},{3,4},{4,5},{5,6},{6,7},{7,8},{8,9},{9,10},{10,1... | collective-permute-start | bytes 1572872 | tf_op jit(solution)/shard_map/ppermute | solution.py:16
  43.8 33.0 %collective-permute-start.5 = (bf16[128,2048]{1,0:T(8,128)(2,1)}, bf16[128,2048]{1,0:T(8,128)(2,1)}, u32[]{:S(2)}, u32[]{:S(2)}) collective-permute-start(bf16[128,2048]{1,0:T(8,128)(2,1)} %collective-permute-done.3), channel_id=1, source_target_pairs={{0,15},{1,0},{2,1},{3,2},{4,3},{5,4},{6,5},{7,6},{8,7},{9,8},{10,9... | collective-permute-start | bytes 1572872 | tf_op jit(solution)/shard_map/ppermute | solution.py:19
  48.3 29.3 %collective-permute-start.6 = (bf16[128,2048]{1,0:T(8,128)(2,1)}, bf16[128,2048]{1,0:T(8,128)(2,1)}, u32[]{:S(2)}, u32[]{:S(2)}) collective-permute-start(bf16[128,2048]{1,0:T(8,128)(2,1)} %collective-permute-done.4), channel_id=1, source_target_pairs={{0,1},{1,2},{2,3},{3,4},{4,5},{5,6},{6,7},{7,8},{8,9},{9,10},{10,1... | collective-permute-start | bytes 1572872 | tf_op jit(solution)/shard_map/ppermute | solution.py:16
  76.8 7.1 %collective-permute-start.7 = (bf16[128,2048]{1,0:T(8,128)(2,1)}, bf16[128,2048]{1,0:T(8,128)(2,1)S(1)}, u32[]{:S(2)}, u32[]{:S(2)}) collective-permute-start(bf16[128,2048]{1,0:T(8,128)(2,1)} %collective-permute-done.5), channel_id=1, source_target_pairs={{0,15},{1,0},{2,1},{3,2},{4,3},{5,4},{6,5},{7,6},{8,7},{9,8},{10,9... | collective-permute-start | bytes 1572872 | tf_op jit(solution)/shard_map/ppermute | solution.py:19
  77.6 12.7 %collective-permute-start.8 = (bf16[128,2048]{1,0:T(8,128)(2,1)}, bf16[128,2048]{1,0:T(8,128)(2,1)S(1)}, u32[]{:S(2)}, u32[]{:S(2)}) collective-permute-start(bf16[128,2048]{1,0:T(8,128)(2,1)} %collective-permute-done.6), channel_id=1, source_target_pairs={{0,1},{1,2},{2,3},{3,4},{4,5},{5,6},{6,7},{7,8},{8,9},{9,10},{10,1... | collective-permute-start | bytes 1572872 | tf_op jit(solution)/shard_map/ppermute | solution.py:16
  83.9 16.1 %collective-permute-start.9 = (bf16[128,2048]{1,0:T(8,128)(2,1)S(1)}, bf16[128,2048]{1,0:T(8,128)(2,1)S(1)}, u32[]{:S(2)}, u32[]{:S(2)}) collective-permute-start(bf16[128,2048]{1,0:T(8,128)(2,1)S(1)} %collective-permute-done.7), channel_id=1, source_target_pairs={{0,15},{1,0},{2,1},{3,2},{4,3},{5,4},{6,5},{7,6},{8,7},{9,8},{10,9... | collective-permute-start | bytes 1572872 | tf_op jit(solution)/shard_map/ppermute | solution.py:19
  90.3 11.4 %collective-permute-start.10 = (bf16[128,2048]{1,0:T(8,128)(2,1)S(1)}, bf16[128,2048]{1,0:T(8,128)(2,1)S(1)}, u32[]{:S(2)}, u32[]{:S(2)}) collective-permute-start(bf16[128,2048]{1,0:T(8,128)(2,1)S(1)} %collective-permute-done.8), channel_id=1, source_target_pairs={{0,1},{1,2},{2,3},{3,4},{4,5},{5,6},{6,7},{7,8},{8,9},{9,10},{10,1... | collective-permute-start | bytes 1572872 | tf_op jit(solution)/shard_map/ppermute | solution.py:16
  99.9 28.6 %copy-start.2 = (f32[2,256,2048]{2,1,0:T(8,128)S(1)}, f32[2,256,2048]{2,1,0:T(8,128)}, u32[]{:S(2)}) copy-start(f32[2,256,2048]{2,1,0:T(8,128)} %fusion.31) | copy-start | bytes 12582916
  100.0 28.6 %copy-start.34 = (pred[2,256]{1,0:T(4,128)(4,1)S(1)}, pred[2,256]{1,0:T(4,128)(4,1)}, u32[]{:S(2)}) copy-start(pred[2,256]{1,0:T(4,128)(4,1)} %copy-done.33) | copy-start | bytes 1540
  100.0 28.6 %copy-start.36 = (bf16[2,256,2048]{2,1,0:T(8,128)(2,1)S(1)}, bf16[2,256,2048]{2,1,0:T(8,128)(2,1)}, u32[]{:S(2)}) copy-start(bf16[2,256,2048]{2,1,0:T(8,128)(2,1)} %param.7) | copy-start | bytes 6291460
  100.0 28.6 %copy-start.37 = (f32[2048]{0:T(1024)S(1)}, f32[2048]{0:T(1024)}, u32[]{:S(2)}) copy-start(f32[2048]{0:T(1024)} %param.11) | copy-start | bytes 24580
  100.0 28.6 %copy-start.38 = (f32[2048]{0:T(1024)S(1)}, f32[2048]{0:T(1024)}, u32[]{:S(2)}) copy-start(f32[2048]{0:T(1024)} %param.12) | copy-start | bytes 24580
  100.0 12.0 %collective-permute-start.11 = (bf16[128,2048]{1,0:T(8,128)(2,1)S(1)}, bf16[128,2048]{1,0:T(8,128)(2,1)S(1)}, u32[]{:S(2)}, u32[]{:S(2)}) collective-permute-start(bf16[128,2048]{1,0:T(8,128)(2,1)S(1)} %collective-permute-done.9), channel_id=1, source_target_pairs={{0,15},{1,0},{2,1},{3,2},{4,3},{5,4},{6,5},{7,6},{8,7},{9,8},{10,9... | collective-permute-start | bytes 1572872 | tf_op jit(solution)/shard_map/ppermute | solution.py:19
  101.7 11.8 %collective-permute-start.12 = (bf16[128,2048]{1,0:T(8,128)(2,1)S(1)}, bf16[128,2048]{1,0:T(8,128)(2,1)S(1)}, u32[]{:S(2)}, u32[]{:S(2)}) collective-permute-start(bf16[128,2048]{1,0:T(8,128)(2,1)S(1)} %collective-permute-done.10), channel_id=1, source_target_pairs={{0,1},{1,2},{2,3},{3,4},{4,5},{5,6},{6,7},{7,8},{8,9},{9,10},{10,1... | collective-permute-start | bytes 1572872 | tf_op jit(solution)/shard_map/ppermute | solution.py:16
  112.0 14.2 %collective-permute-start.13 = (bf16[128,2048]{1,0:T(8,128)(2,1)S(1)}, bf16[128,2048]{1,0:T(8,128)(2,1)S(1)}, u32[]{:S(2)}, u32[]{:S(2)}) collective-permute-start(bf16[128,2048]{1,0:T(8,128)(2,1)S(1)} %collective-permute-done.11), channel_id=1, source_target_pairs={{0,15},{1,0},{2,1},{3,2},{4,3},{5,4},{6,5},{7,6},{8,7},{9,8},{10,9... | collective-permute-start | bytes 1572872 | tf_op jit(solution)/shard_map/ppermute | solution.py:19
  113.5 14.2 %collective-permute-start.14 = (bf16[128,2048]{1,0:T(8,128)(2,1)S(1)}, bf16[128,2048]{1,0:T(8,128)(2,1)S(1)}, u32[]{:S(2)}, u32[]{:S(2)}) collective-permute-start(bf16[128,2048]{1,0:T(8,128)(2,1)S(1)} %collective-permute-done.12), channel_id=1, source_target_pairs={{0,1},{1,2},{2,3},{3,4},{4,5},{5,6},{6,7},{7,8},{8,9},{9,10},{10,1... | collective-permute-start | bytes 1572872 | tf_op jit(solution)/shard_map/ppermute | solution.py:16
  159.9 238.6 %reduce-scatter.3.cloned.1.call-start = ((), (), s32[]{:S(2)}) async-start(), calls=%async_computation.2 | async-start | bytes 17825792 | tf_op jit(solution)/shard_map/reduce_scatter | solution.py:113
  173.7 12.7 %copy-start.4 = (f32[1,2048]{1,0:T(1,128)S(1)}, f32[1,2048]{1,0:T(1,128)}, u32[]{:S(2)}) copy-start(f32[1,2048]{1,0:T(1,128)} %get-tuple-element.44) | copy-start | bytes 24580
  173.7 12.7 %copy-start.5 = (f32[1,2048]{1,0:T(1,128)S(1)}, f32[1,2048]{1,0:T(1,128)}, u32[]{:S(2)}) copy-start(f32[1,2048]{1,0:T(1,128)} %get-tuple-element.45) | copy-start | bytes 24580
  173.7 12.7 %copy-start.6 = (f32[1,2048]{1,0:T(1,128)S(1)}, f32[1,2048]{1,0:T(1,128)}, u32[]{:S(2)}) copy-start(f32[1,2048]{1,0:T(1,128)} %get-tuple-element.46) | copy-start | bytes 24580
  173.7 12.7 %copy-start.7 = (f32[1,2048]{1,0:T(1,128)S(1)}, f32[1,2048]{1,0:T(1,128)}, u32[]{:S(2)}) copy-start(f32[1,2048]{1,0:T(1,128)} %get-tuple-element.47) | copy-start | bytes 24580
  173.7 12.7 %copy-start.8 = (f32[1,2048]{1,0:T(1,128)S(1)}, f32[1,2048]{1,0:T(1,128)}, u32[]{:S(2)}) copy-start(f32[1,2048]{1,0:T(1,128)} %get-tuple-element.48) | copy-start | bytes 24580
  173.7 12.7 %copy-start.9 = (f32[1,2048]{1,0:T(1,128)S(1)}, f32[1,2048]{1,0:T(1,128)}, u32[]{:S(2)}) copy-start(f32[1,2048]{1,0:T(1,128)} %get-tuple-element.49) | copy-start | bytes 24580
  173.7 12.7 %copy-start.10 = (f32[1,2048]{1,0:T(1,128)S(1)}, f32[1,2048]{1,0:T(1,128)}, u32[]{:S(2)}) copy-start(f32[1,2048]{1,0:T(1,128)} %get-tuple-element.50) | copy-start | bytes 24580
  173.7 12.7 %copy-start.11 = (f32[1,2048]{1,0:T(1,128)S(1)}, f32[1,2048]{1,0:T(1,128)}, u32[]{:S(2)}) copy-start(f32[1,2048]{1,0:T(1,128)} %get-tuple-element.51) | copy-start | bytes 24580
  173.8 12.7 %copy-start.12 = (f32[1,2048]{1,0:T(1,128)S(1)}, f32[1,2048]{1,0:T(1,128)}, u32[]{:S(2)}) copy-start(f32[1,2048]{1,0:T(1,128)} %get-tuple-element.52) | copy-start | bytes 24580
  173.8 12.7 %copy-start.13 = (f32[1,2048]{1,0:T(1,128)S(1)}, f32[1,2048]{1,0:T(1,128)}, u32[]{:S(2)}) copy-start(f32[1,2048]{1,0:T(1,128)} %get-tuple-element.53) | copy-start | bytes 24580
  173.8 12.7 %copy-start.14 = (f32[1,2048]{1,0:T(1,128)S(1)}, f32[1,2048]{1,0:T(1,128)}, u32[]{:S(2)}) copy-start(f32[1,2048]{1,0:T(1,128)} %get-tuple-element.54) | copy-start | bytes 24580
  173.8 12.7 %copy-start.15 = (f32[1,2048]{1,0:T(1,128)S(1)}, f32[1,2048]{1,0:T(1,128)}, u32[]{:S(2)}) copy-start(f32[1,2048]{1,0:T(1,128)} %get-tuple-element.55) | copy-start | bytes 24580
  173.8 12.7 %copy-start.16 = (f32[1,2048]{1,0:T(1,128)S(1)}, f32[1,2048]{1,0:T(1,128)}, u32[]{:S(2)}) copy-start(f32[1,2048]{1,0:T(1,128)} %get-tuple-element.56) | copy-start | bytes 24580
  173.8 12.7 %copy-start.17 = (f32[1,2048]{1,0:T(1,128)S(1)}, f32[1,2048]{1,0:T(1,128)}, u32[]{:S(2)}) copy-start(f32[1,2048]{1,0:T(1,128)} %get-tuple-element.57) | copy-start | bytes 24580
  173.8 12.7 %copy-start.18 = (f32[1,2048]{1,0:T(1,128)S(1)}, f32[1,2048]{1,0:T(1,128)}, u32[]{:S(2)}) copy-start(f32[1,2048]{1,0:T(1,128)} %get-tuple-element.58) | copy-start | bytes 24580
  173.8 12.7 %copy-start.19 = (f32[1,2048]{1,0:T(1,128)S(1)}, f32[1,2048]{1,0:T(1,128)}, u32[]{:S(2)}) copy-start(f32[1,2048]{1,0:T(1,128)} %get-tuple-element.59) | copy-start | bytes 24580
  173.8 12.7 %copy-start.20 = (f32[1,2048]{1,0:T(1,128)S(1)}, f32[1,2048]{1,0:T(1,128)}, u32[]{:S(2)}) copy-start(f32[1,2048]{1,0:T(1,128)} %get-tuple-element.60) | copy-start | bytes 24580
  173.8 12.7 %copy-start.21 = (f32[1,2048]{1,0:T(1,128)S(1)}, f32[1,2048]{1,0:T(1,128)}, u32[]{:S(2)}) copy-start(f32[1,2048]{1,0:T(1,128)} %get-tuple-element.61) | copy-start | bytes 24580
  173.9 12.7 %copy-start.22 = (f32[1,2048]{1,0:T(1,128)S(1)}, f32[1,2048]{1,0:T(1,128)}, u32[]{:S(2)}) copy-start(f32[1,2048]{1,0:T(1,128)} %get-tuple-element.62) | copy-start | bytes 24580
  173.9 12.7 %copy-start.23 = (f32[1,2048]{1,0:T(1,128)S(1)}, f32[1,2048]{1,0:T(1,128)}, u32[]{:S(2)}) copy-start(f32[1,2048]{1,0:T(1,128)} %get-tuple-element.63) | copy-start | bytes 24580
  173.9 12.7 %copy-start.24 = (f32[1,2048]{1,0:T(1,128)S(1)}, f32[1,2048]{1,0:T(1,128)}, u32[]{:S(2)}) copy-start(f32[1,2048]{1,0:T(1,128)} %get-tuple-element.64) | copy-start | bytes 24580
  175.3 10.0 %collective-permute-start.17 = (bf16[2,15,2048]{2,1,0:T(8,128)(2,1)S(1)}, bf16[2,15,2048]{2,1,0:T(8,128)(2,1)S(1)}, u32[]{:S(2)}, u32[]{:S(2)}) collective-permute-start(bf16[2,15,2048]{2,1,0:T(8,128)(2,1)S(1)} %get-tuple-element.38), channel_id=1, source_target_pairs={{1,0},{2,1},{3,2},{4,3},{5,4},{6,5},{7,6},{8,7},{9,8},{10,9},{11,1... | collective-permute-start | bytes 368648 | tf_op jit(solution)/shard_map/ppermute | solution.py:34
  176.6 9.7 %collective-permute-start.18 = (bf16[2,15,2048]{2,1,0:T(8,128)(2,1)S(1)}, bf16[2,15,2048]{2,1,0:T(8,128)(2,1)S(1)}, u32[]{:S(2)}, u32[]{:S(2)}) collective-permute-start(bf16[2,15,2048]{2,1,0:T(8,128)(2,1)S(1)} %get-tuple-element.39), channel_id=1, source_target_pairs={{0,1},{1,2},{2,3},{3,4},{4,5},{5,6},{6,7},{7,8},{8,9},{9,10},{10,1... | collective-permute-start | bytes 368648 | tf_op jit(solution)/shard_map/ppermute | solution.py:31
  (12 other events, 125.2 us)
Sparse Core Ops, SparseCore 0:
  160.0 57.2 reduce-scatter.4
  222.0 176.3 reduce-scatter.2
